TPU v7x, 128 devices: a whole 4x4x4 slice. The times are simulated.
128 devices in a mesh: section: 4 (over z), space: 32 (over x, y, core).
Axes of the slice: x: 4, y: 4, z: 4, core: 2. Of those that a mesh axis runs over, the one named last changes fastest.
Arguments:
- features: bfloat16 [4, 128, 784, 256], P('section', 'space')
- tissue: int32 [4, 128], P('section'), may hold values from 0 to 1, as said below
- first_weight: bfloat16 [256, 512], replicated, may hold values from -0.375 to 0.375
- first_gain: float32 [512], replicated, may hold values from 0.1 to 1.9
- first_bias: float32 [512], replicated, may hold values from -3 to 3
- second_weight: bfloat16 [512, 1024], P(None, 'space'), may hold values from -0.25 to 0.25
- second_gain: float32 [1024], replicated, may hold values from 0.1 to 1.9
- second_bias: float32 [1024], replicated, may hold values from -3 to 3
Outputs:
- output: bfloat16 [4, 1024, 100352], P('section', 'space')
- first_mean: float32 [512], replicated
- first_var: float32 [512], replicated
- second_mean: float32 [1024], P('space')
- second_var: float32 [1024], P('space')
Inputs may be any that keep to these rules, and one draw needn't show every extreme that they name: Every tile row holds at least one tissue tile and at least one tile without tissue.
All inputs are finite; a program needn't handle non-finite values.
Results may differ from a plain program's by a relative error of at most 0.0053.
Values may be sent and summed in bfloat16 or wider, within the bound.
No kernel may reach another device: no remote copies, remote signals or barrier semaphores. Data moves between devices by JAX's collectives and lax.ppermute only.
A program may use at most 128 MiB of HBM per device.

v0:
```python
import jax
import jax.numpy as jnp
from jax import lax
from jax.sharding import PartitionSpec as P

EPS = 1e-05


def normalize(values, mean_val, var_val, gain, bias):
    return jnp.maximum(gain * (values - mean_val) * lax.rsqrt(var_val + EPS) + bias, 0.0)


def masked_sum(values, weight):
    return jnp.sum(values * weight, axis=(0, 1, 2))


def masked_squares(values, weight, mean_val):
    centred = values - mean_val
    return jnp.sum(weight * centred * centred, axis=(0, 1, 2))


def channel_first(values):
    batch, tiles_here, pixels, chans = values.shape
    return jnp.transpose(values, (0, 3, 1, 2)).reshape(batch, chans, tiles_here * pixels)


def shards(
    features, tissue, first_weight, first_gain, first_bias, second_weight, second_gain, second_bias
):
    index = lax.axis_index("space")
    tiles_here = features.shape[1]
    pixels = features.shape[2]
    row_mask = tissue[0].astype(jnp.float32)
    own_mask = lax.dynamic_slice_in_dim(row_mask, index * tiles_here, tiles_here)
    own_weight = own_mask[None, :, None, None]
    local_count = jnp.sum(own_mask) * pixels
    first = jnp.einsum("mtpc,cd->mtpd", features, first_weight, preferred_element_type=jnp.float32)
    total, count = lax.psum((masked_sum(first, own_weight), local_count), ("section", "space"))
    first_mean = total / count
    first_var = (
        lax.psum(masked_squares(first, own_weight, first_mean), ("section", "space")) / count
    )
    activation = normalize(first, first_mean, first_var, first_gain, first_bias).astype(
        jnp.bfloat16
    )
    second = jnp.einsum(
        "mtpc,cd->mtpd",
        activation,
        lax.all_gather(second_weight, "space", axis=1, tiled=True),
        preferred_element_type=jnp.float32,
    )
    width_here = second_weight.shape[1]
    moved = lax.all_to_all(channel_first(second), "space", split_axis=1, concat_axis=2, tiled=True)
    row_weight = jnp.repeat(row_mask, pixels)[None, None, :]
    second_mean = lax.psum(jnp.sum(moved * row_weight, axis=(0, 2)), "section") / count
    centred = moved - second_mean[:, None]
    second_var = lax.psum(jnp.sum(row_weight * centred * centred, axis=(0, 2)), "section") / count
    gain_here = lax.dynamic_slice_in_dim(second_gain, index * width_here, width_here)
    bias_here = lax.dynamic_slice_in_dim(second_bias, index * width_here, width_here)
    output = normalize(
        moved, second_mean[:, None], second_var[:, None], gain_here[:, None], bias_here[:, None]
    ).astype(jnp.bfloat16)
    return (output, first_mean, first_var, second_mean, second_var)


def solution(mesh):
    in_specs = (
        P("section", "space", None, None),
        P("section", None),
        P(),
        P(),
        P(),
        P(None, "space"),
        P(),
        P(),
    )
    out_specs = (P("section", "space", None), P(), P(), P("space"), P("space"))
    return jax.shard_map(shards, mesh=mesh, in_specs=in_specs, out_specs=out_specs, check_vma=False)
```

profile of v0, /device:TPU:44, one launch (start us, length us, event | category | flops | bytes accessed | tf_op | source)
XLA Modules:
  0.0 490.6 jit_solution(13047732161503273822)
XLA Ops:
  7.2 0.0 copy-start
  7.2 0.0 all-gather.2.cloned.1.call-start
  7.2 0.7 all-gather.2.cloned.1.call-update
  7.9 0.7 convert_element_type.23
  8.6 0.7 fusion.12
  9.9 0.0 copy-done
  9.9 4.7 multiply_reduce_fusion.1
  14.6 0.0 copy-start.4
  14.6 0.0 copy-start.5
  14.6 64.0 %all-reduce = (f32[512]{0:T(512)S(1)}, f32[]{:T(128)}) all-reduce(f32[512]{0:T(512)S(1)} %get-tuple-element.13, f32[]{:T(128)S(6)} %mul.112), channel_id=1, replica_groups=mesh['section'=4,'space'=32] {'section','space'}, use_global_device_ids=true, to_apply=%region_1.0 | all-reduce | flops 513 | bytes 4104 | tf_op jit(solution)/shard_map/psum | solution.py:38
  78.6 0.7 broadcast_divide_fusion.1
  79.3 0.0 copy-start.2
  79.3 3.9 fusion.1
  83.2 62.5 %psum.37 = f32[512]{0:T(512)S(1)} all-reduce(f32[512]{0:T(512)S(1)} %fusion.1), channel_id=1, replica_groups=mesh['section'=4,'space'=32] {'section','space'}, use_global_device_ids=true, to_apply=%region_5.0 | all-reduce | flops 512 | bytes 4096 | tf_op jit(solution)/shard_map/psum | solution.py:41
  145.7 1.3 add_rsqrt_fusion
  147.0 0.0 all-gather.2.cloned.1.call-done
  147.0 0.0 copy-done.4
  147.0 0.0 copy-done.5
  147.0 11.2 %fusion.2 = f32[4,784,1024]{2,1,0:T(8,128)} fusion(f32[4,784,512]{2,1,0:T(8,128)} %get-tuple-element.14, f32[512]{0:T(512)S(1)} %copy-done.4, f32[512]{0:T(512)S(1)} %get-tuple-element.9, f32[512]{0:T(512)S(1)} %broadcast_divide_fusion.1, f32[512]{0:T(512)S(1)} %copy-done.5, bf16[512,1024]{0,1:T(8,128)(2,1)} %all-gather.2.cloned.1.call-done), kind=kOutput, calls=%fused_computation.8 | convolution fusion | flops 3297968128 | bytes 20324352 | tf_op jit(solution)/shard_map/mtpc,cd->mtpd/dot_general | solution.py:46
  158.2 0.0 copy-done.2
  158.2 27.1 %copy.17 = f32[1,1024,3136]{2,0,1:T(1,128)} copy(f32[1,1024,3136]{1,2,0:T(8,128)} %bitcast.28) | data formatting | bytes 25690112 | tf_op jit(solution)/shard_map/reshape | solution.py:24
  185.3 0.0 copy-start.6
  185.3 8.8 %all-to-all-start = ((f32[1,1024,3136]{2,0,1:T(1,128)}), f32[1,1024,3136]{2,0,1:T(1,128)}, u32[]{:S(2)}, u32[]{:S(2)}) async-start(f32[1,1024,3136]{2,0,1:T(1,128)} %copy.17), calls=%async_computation | async-start | bytes 26214400 | tf_op jit(solution)/shard_map/all_to_all | solution.py:53
  194.1 0.0 copy-done.6
  194.1 0.1 convert_element_type.25
  194.2 0.1 broadcast_in_dim.4
  194.4 0.3 broadcast_in_dim.5
  194.6 0.8 dynamic_slice.11
  195.4 0.8 dynamic_slice.14
  196.2 204.3 %all-to-all-done = f32[1,1024,3136]{2,0,1:T(1,128)} async-done(((f32[1,1024,3136]{2,0,1:T(1,128)}), f32[1,1024,3136]{2,0,1:T(1,128)}, u32[]{:S(2)}, u32[]{:S(2)}) %all-to-all-start) | async-done | bytes 12845088 | tf_op jit(solution)/shard_map/all_to_all | solution.py:53
  400.4 10.3 %copy.19 = f32[1,1024,3136]{2,1,0:T(8,128)} copy(f32[1,1024,3136]{2,0,1:T(1,128)} %all-to-all-done) | data formatting | bytes 25690112
  410.7 17.0 %copy.18 = f32[1,32,32,3136]{3,2,1,0:T(8,128)} copy(f32[1,32,32,3136]{3,1,2,0:T(8,128)} %bitcast.25) | data formatting | bytes 25690112 | tf_op jit(solution)/shard_map/all_to_all | solution.py:53
  427.7 5.7 %multiply_reduce_fusion = f32[32]{0:T(128)S(1)} fusion(f32[1,32,32,3136]{3,1,2,0:T(8,128)} %bitcast.26, f32[32,3136]{1,0:T(8,128)S(1)} %broadcast_in_dim.5), kind=kLoop, calls=%fused_computation.2 | loop fusion | flops 6422496 | bytes 13246592 | tf_op jit(solution)/shard_map/reduce_sum | solution.py:55
  433.4 9.0 %psum.38 = f32[32]{0:T(128)S(1)} all-reduce(f32[32]{0:T(128)S(1)} %multiply_reduce_fusion), channel_id=1, replica_groups=mesh['section'=4,'space'=32] {'section'}, use_global_device_ids=true, to_apply=%region_7.0 | all-reduce | flops 32 | bytes 256 | tf_op jit(solution)/shard_map/psum | solution.py:55
  442.4 0.7 broadcast_divide_fusion.3
  443.1 0.0 copy-start.3
  443.1 6.6 %fusion = f32[32]{0:T(128)S(1)} fusion(f32[1,32,32,3136]{3,1,2,0:T(8,128)} %bitcast.27, f32[32]{0:T(128)S(1)} %broadcast_divide_fusion.3, f32[32,3136]{1,0:T(8,128)S(1)} %broadcast_in_dim.5), kind=kLoop, calls=%fused_computation.1 | loop fusion | flops 12845024 | bytes 13246720 | tf_op jit(solution)/shard_map/reduce_sum | solution.py:57
  449.7 9.9 %psum.39 = f32[32]{0:T(128)S(1)} all-reduce(f32[32]{0:T(128)S(1)} %fusion), channel_id=1, replica_groups=mesh['section'=4,'space'=32] {'section'}, use_global_device_ids=true, to_apply=%region_9.0 | all-reduce | flops 32 | bytes 256 | tf_op jit(solution)/shard_map/psum | solution.py:57
  459.6 1.2 add_rsqrt_fusion.1
  460.8 12.9 %all_to_all.16 = f32[1,32,100352]{2,1,0:T(8,128)} reshape(f32[1,32,32,3136]{3,2,1,0:T(8,128)} %copy.18) | data formatting | bytes 25690112 | tf_op jit(solution)/shard_map/all_to_all | solution.py:53
  473.7 0.0 copy-start.1
  473.7 0.0 copy-done.3
  473.7 10.0 %maximum_convert_fusion = bf16[1,32,100352]{2,1,0:T(8,128)(2,1)} fusion(f32[1,32,100352]{2,1,0:T(8,128)} %all_to_all.16, f32[32]{0:T(128)S(1)} %dynamic_slice.14, f32[32]{0:T(128)S(1)} %get-tuple-element.7, f32[32]{0:T(128)S(1)} %broadcast_divide_fusion.3, f32[32]{0:T(128)S(1)} %dynamic_slice.11), kind=kLoop, calls=%fused_computation.3 | loop fusion | flops 19267584 | bytes 19268096 | tf_op jit(solution)/shard_map/convert_element_type | solution.py:62
  483.7 0.0 copy-done.1
  (1 shorter events, 0.0 us)
Async XLA Ops:
  7.2 2.7 copy-start
  7.2 139.8 %all-gather.2.cloned.1.call-start = ((), (), s32[]{:S(2)}) async-start(), calls=%async_computation.1 | async-start | bytes 1081344 | tf_op jit(solution)/shard_map/all_gather | solution.py:49
  14.6 132.3 %copy-start.4 = (f32[512]{0:T(512)S(1)}, f32[512]{0:T(512)}, u32[]{:S(2)}) copy-start(f32[512]{0:T(512)} %param.12) | copy-start | bytes 6148
  14.6 132.4 %copy-start.5 = (f32[512]{0:T(512)S(1)}, f32[512]{0:T(512)}, u32[]{:S(2)}) copy-start(f32[512]{0:T(512)} %param.11) | copy-start | bytes 6148
  79.3 78.9 %copy-start.2 = (f32[512]{0:T(512)}, f32[512]{0:T(512)S(1)}, u32[]{:S(2)}) copy-start(f32[512]{0:T(512)S(1)} %broadcast_divide_fusion.1) | copy-start | bytes 6148
  185.3 8.8 %copy-start.6 = (s32[1,128]{1,0:T(1,128)S(1)}, s32[1,128]{1,0:T(1,128)}, u32[]{:S(2)}) copy-start(s32[1,128]{1,0:T(1,128)} %param.9) | copy-start | bytes 1540
  185.3 215.1 %all-to-all-start = ((f32[1,1024,3136]{2,0,1:T(1,128)}), f32[1,1024,3136]{2,0,1:T(1,128)}, u32[]{:S(2)}, u32[]{:S(2)}) async-start(f32[1,1024,3136]{2,0,1:T(1,128)} %copy.17), calls=%async_computation | async-start | bytes 26214400 | tf_op jit(solution)/shard_map/all_to_all | solution.py:53
  443.1 30.7 %copy-start.3 = (f32[32]{0:T(128)}, f32[32]{0:T(128)S(1)}, u32[]{:S(2)}) copy-start(f32[32]{0:T(128)S(1)} %broadcast_divide_fusion.3) | copy-start | bytes 388
  473.7 10.0 %copy-start.1 = (bf16[1,4,784,256]{3,2,1,0:T(8,128)(2,1)S(1)}, bf16[1,4,784,256]{3,2,1,0:T(8,128)(2,1)}, u32[]{:S(2)}) copy-start(bf16[1,4,784,256]{3,2,1,0:T(8,128)(2,1)} %param.8) | copy-start | bytes 4816900
Sparse Core Ops, SparseCore 0:
  10.3 42.4 all-gather.1
where the time goes:
time: 492 us; the launch traced here: 491 us
  waiting for transfers between devices  205 us (42%)
  blocking collectives  145 us (29%)
  local copies, waits for them, and re-layouts  69.3 us (14%)
  other arithmetic  31.4 us (6%)
  matrix products  15.9 us (3%)
  between operations  14.8 us (3%)
  starting transfers between devices  8.84 us (2%)
    all_to_all x1, waiting for transfers between devices, shards(): lax.all_to_all(channel_first(second), 'space', split_axis=1, concat_axis=...  204 us
    psum x1, blocking collectives, shards(): lax.psum((masked_sum(first, own_weight), local_count), ('section', 'space'))  64 us
    psum x1, blocking collectives, shards(): lax.psum(masked_squares(first, own_weight, first_mean), ('section', 'spac...  62.5 us
    all_to_all x2, local copies, waits for them, and re-layouts, shards(): lax.all_to_all(channel_first(second), 'space', split_axis=1, concat_axis=...  29.9 us
    reshape x1, local copies, waits for them, and re-layouts, channel_first(): jnp.transpose(values, (0, 3, 1, 2))  27.1 us
    dot_general x1, matrix products, shards(): jnp.einsum('mtpc,cd->mtpd', activation, lax.all_gather(second_weight, 'sp...  11.2 us
    unnamed x15, local copies, waits for them, and re-layouts  10.3 us
    convert_element_type x1, other arithmetic, shards(): output = normalize(moved, second_mean[:, None], second_var[:, None], gain...  9.96 us
  transfers between devices with their start and end apart: 2, of which 1 were waited for; matrix products, arithmetic and copies ran while one was open for 3% of the time, Pallas kernels for 0%

commit v1 on v0

--- a/solution.py
+++ b/solution.py
@@ -4,6 +4,10 @@
 from jax.sharding import PartitionSpec as P
 
 EPS = 1e-05
+
+
+def refer_area(local_array, row_axis):
+    return lax.all_gather(local_array, axis_name=row_axis).sum(axis=0)
 
 
 def normalize(values, mean_val, var_val, gain, bias):
@@ -38,7 +42,7 @@
     total, count = lax.psum((masked_sum(first, own_weight), local_count), ("section", "space"))
     first_mean = total / count
     first_var = (
-        lax.psum(masked_squares(first, own_weight, first_mean), ("section", "space")) / count
+        refer_area(masked_squares(first, own_weight, first_mean), ("section", "space")) / count
     )
     activation = normalize(first, first_mean, first_var, first_gain, first_bias).astype(
         jnp.bfloat16

time: 492 us -> 463 us (0.941)
  blocking collectives: 145 us -> 116 us
    psum x1 -> x0, blocking collectives: 62.5 us -> none  [shards(): lax.psum(masked_squares(first, own_weight, first_mean), ('section', 'spac...]
    all_gather x0 -> x1, blocking collectives: none -> 33.3 us  [refer_area(): return lax.all_gather(local_array, axis_name=row_axis).sum(axis=0)]
where the time goes in v1:
time: 463 us; the launch traced here: 460 us
  waiting for transfers between devices  205 us (44%)
  blocking collectives  116 us (25%)
  local copies, waits for them, and re-layouts  69.3 us (15%)
  other arithmetic  31.6 us (7%)
  matrix products  15.9 us (3%)
  between operations  14.8 us (3%)
  starting transfers between devices  7.81 us (2%)
    all_to_all x1, waiting for transfers between devices, shards(): lax.all_to_all(channel_first(second), 'space', split_axis=1, concat_axis=...  204 us
    psum x1, blocking collectives, shards(): lax.psum((masked_sum(first, own_weight), local_count), ('section', 'space'))  64 us
    all_gather x1, blocking collectives, refer_area(): return lax.all_gather(local_array, axis_name=row_axis).sum(axis=0)  33.3 us
    all_to_all x2, local copies, waits for them, and re-layouts, shards(): lax.all_to_all(channel_first(second), 'space', split_axis=1, concat_axis=...  29.9 us
    reshape x1, local copies, waits for them, and re-layouts, channel_first(): jnp.transpose(values, (0, 3, 1, 2))  27.1 us
    dot_general x1, matrix products, shards(): jnp.einsum('mtpc,cd->mtpd', activation, lax.all_gather(second_weight, 'sp...  11.2 us
    unnamed x15, local copies, waits for them, and re-layouts  10.3 us
    psum x1, blocking collectives, shards(): lax.psum(jnp.sum(moved * row_weight, axis=(0, 2)), 'section') / count  10.2 us
  transfers between devices with their start and end apart: 2, of which 1 were waited for; matrix products, arithmetic and copies ran while one was open for 3% of the time, Pallas kernels for 0%

profile of v1, /device:TPU:44, one launch (start us, length us, event | category | flops | bytes accessed | tf_op | source)
XLA Modules:
  0.0 460.5 jit_solution(10540511541668194254)
XLA Ops:
  7.2 0.0 copy-start
  7.2 0.0 all-gather.4.cloned.1.call-start
  7.2 0.7 all-gather.4.cloned.1.call-update
  7.9 0.7 convert_element_type.23
  8.6 0.7 fusion.12
  9.9 0.0 copy-done
  9.9 4.7 %multiply_reduce_fusion.1 = (f32[512]{0:T(512)S(1)}, f32[4,784,512]{2,1,0:T(8,128)}) fusion(f32[4]{0:T(128)S(1)} %get-tuple-element.12, bf16[256,512]{1,0:T(8,128)(2,1)} %param.10, bf16[1,4,784,256]{3,2,1,0:T(8,128)(2,1)S(1)} %copy-done), kind=kOutput, calls=%fused_computation.7 | convolution fusion | flops 825294336 | bytes 8292368 | tf_op jit(solution)/shard_map/mtpc,cd->mtpd/dot_general | solution.py:41
  14.6 0.0 copy-start.4
  14.6 0.0 copy-start.5
  14.6 64.0 %all-reduce = (f32[512]{0:T(512)S(1)}, f32[]{:T(128)}) all-reduce(f32[512]{0:T(512)S(1)} %get-tuple-element.13, f32[]{:T(128)S(6)} %mul.112), channel_id=1, replica_groups=mesh['section'=4,'space'=32] {'section','space'}, use_global_device_ids=true, to_apply=%region_1.0 | all-reduce | flops 513 | bytes 4104 | tf_op jit(solution)/shard_map/psum | solution.py:42
  78.6 0.7 broadcast_divide_fusion.1
  79.3 0.0 copy-start.2
  79.3 3.9 fusion.1
  83.2 33.3 %all-gather.1 = f32[128,1,512]{2,1,0:T(1,128)S(1)} all-gather(f32[1,1,512]{2,1,0:T(1,128)S(1)} %bitcast.30), channel_id=2, replica_groups=mesh['section'=4,'space'=32] {'section','space'}, dimensions={0}, use_global_device_ids=true | all-gather | bytes 264192 | tf_op jit(solution)/shard_map/all_gather | solution.py:10
  116.5 0.2 reduce_sum.57
  116.7 1.3 add_rsqrt_fusion
  118.0 0.0 all-gather.4.cloned.1.call-done
  118.0 0.0 copy-done.4
  118.0 0.0 copy-done.5
  118.0 11.2 %fusion.2 = f32[4,784,1024]{2,1,0:T(8,128)} fusion(f32[4,784,512]{2,1,0:T(8,128)} %get-tuple-element.14, f32[512]{0:T(512)S(1)} %copy-done.4, f32[512]{0:T(512)S(1)} %get-tuple-element.9, f32[512]{0:T(512)S(1)} %broadcast_divide_fusion.1, f32[512]{0:T(512)S(1)} %copy-done.5, bf16[512,1024]{0,1:T(8,128)(2,1)} %all-gather.4.cloned.1.call-done), kind=kOutput, calls=%fused_computation.8 | convolution fusion | flops 3297968128 | bytes 20324352 | tf_op jit(solution)/shard_map/mtpc,cd->mtpd/dot_general | solution.py:50
  129.3 0.0 copy-done.2
  129.3 27.1 %copy.17 = f32[1,1024,3136]{2,0,1:T(1,128)} copy(f32[1,1024,3136]{1,2,0:T(8,128)} %bitcast.29) | data formatting | bytes 25690112 | tf_op jit(solution)/shard_map/reshape | solution.py:28
  156.3 0.0 copy-start.6
  156.3 7.8 %all-to-all-start = ((f32[1,1024,3136]{2,0,1:T(1,128)}), f32[1,1024,3136]{2,0,1:T(1,128)}, u32[]{:S(2)}, u32[]{:S(2)}) async-start(f32[1,1024,3136]{2,0,1:T(1,128)} %copy.17), calls=%async_computation | async-start | bytes 26214400 | tf_op jit(solution)/shard_map/all_to_all | solution.py:57
  164.1 0.0 copy-done.6
  164.2 0.1 convert_element_type.25
  164.3 0.1 broadcast_in_dim.4
  164.4 0.3 broadcast_in_dim.5
  164.7 0.8 dynamic_slice.11
  165.4 0.8 dynamic_slice.14
  166.2 204.1 %all-to-all-done = f32[1,1024,3136]{2,0,1:T(1,128)} async-done(((f32[1,1024,3136]{2,0,1:T(1,128)}), f32[1,1024,3136]{2,0,1:T(1,128)}, u32[]{:S(2)}, u32[]{:S(2)}) %all-to-all-start) | async-done | bytes 12845088 | tf_op jit(solution)/shard_map/all_to_all | solution.py:57
  370.3 10.3 %copy.19 = f32[1,1024,3136]{2,1,0:T(8,128)} copy(f32[1,1024,3136]{2,0,1:T(1,128)} %all-to-all-done) | data formatting | bytes 25690112
  380.6 17.0 %copy.18 = f32[1,32,32,3136]{3,2,1,0:T(8,128)} copy(f32[1,32,32,3136]{3,1,2,0:T(8,128)} %bitcast.26) | data formatting | bytes 25690112 | tf_op jit(solution)/shard_map/all_to_all | solution.py:57
  397.6 5.7 %multiply_reduce_fusion = f32[32]{0:T(128)S(1)} fusion(f32[1,32,32,3136]{3,1,2,0:T(8,128)} %bitcast.27, f32[32,3136]{1,0:T(8,128)S(1)} %broadcast_in_dim.5), kind=kLoop, calls=%fused_computation.2 | loop fusion | flops 6422496 | bytes 13246592 | tf_op jit(solution)/shard_map/reduce_sum | solution.py:59
  403.3 10.2 %psum.30 = f32[32]{0:T(128)S(1)} all-reduce(f32[32]{0:T(128)S(1)} %multiply_reduce_fusion), channel_id=1, replica_groups=mesh['section'=4,'space'=32] {'section'}, use_global_device_ids=true, to_apply=%region_7.0 | all-reduce | flops 32 | bytes 256 | tf_op jit(solution)/shard_map/psum | solution.py:59
  413.4 0.7 broadcast_divide_fusion.3
  414.1 0.0 copy-start.3
  414.2 6.6 %fusion = f32[32]{0:T(128)S(1)} fusion(f32[1,32,32,3136]{3,1,2,0:T(8,128)} %bitcast.28, f32[32]{0:T(128)S(1)} %broadcast_divide_fusion.3, f32[32,3136]{1,0:T(8,128)S(1)} %broadcast_in_dim.5), kind=kLoop, calls=%fused_computation.1 | loop fusion | flops 12845024 | bytes 13246720 | tf_op jit(solution)/shard_map/reduce_sum | solution.py:61
  420.8 8.8 %psum.31 = f32[32]{0:T(128)S(1)} all-reduce(f32[32]{0:T(128)S(1)} %fusion), channel_id=1, replica_groups=mesh['section'=4,'space'=32] {'section'}, use_global_device_ids=true, to_apply=%region_9.0 | all-reduce | flops 32 | bytes 256 | tf_op jit(solution)/shard_map/psum | solution.py:61
  429.5 1.2 add_rsqrt_fusion.1
  430.8 12.9 %all_to_all.16 = f32[1,32,100352]{2,1,0:T(8,128)} reshape(f32[1,32,32,3136]{3,2,1,0:T(8,128)} %copy.18) | data formatting | bytes 25690112 | tf_op jit(solution)/shard_map/all_to_all | solution.py:57
  443.6 0.0 copy-start.1
  443.6 0.0 copy-done.3
  443.7 10.0 %maximum_convert_fusion = bf16[1,32,100352]{2,1,0:T(8,128)(2,1)} fusion(f32[1,32,100352]{2,1,0:T(8,128)} %all_to_all.16, f32[32]{0:T(128)S(1)} %dynamic_slice.14, f32[32]{0:T(128)S(1)} %get-tuple-element.7, f32[32]{0:T(128)S(1)} %broadcast_divide_fusion.3, f32[32]{0:T(128)S(1)} %dynamic_slice.11), kind=kLoop, calls=%fused_computation.3 | loop fusion | flops 19267584 | bytes 19268096 | tf_op jit(solution)/shard_map/convert_element_type | solution.py:66
  453.6 0.0 copy-done.1
  (1 shorter events, 0.0 us)
Async XLA Ops:
  7.2 2.7 copy-start
  7.2 110.8 %all-gather.4.cloned.1.call-start = ((), (), s32[]{:S(2)}) async-start(), calls=%async_computation.1 | async-start | bytes 1081344 | tf_op jit(solution)/shard_map/all_gather | solution.py:53
  14.6 103.4 %copy-start.4 = (f32[512]{0:T(512)S(1)}, f32[512]{0:T(512)}, u32[]{:S(2)}) copy-start(f32[512]{0:T(512)} %param.12) | copy-start | bytes 6148
  14.6 103.4 %copy-start.5 = (f32[512]{0:T(512)S(1)}, f32[512]{0:T(512)}, u32[]{:S(2)}) copy-start(f32[512]{0:T(512)} %param.11) | copy-start | bytes 6148
  79.3 50.0 %copy-start.2 = (f32[512]{0:T(512)}, f32[512]{0:T(512)S(1)}, u32[]{:S(2)}) copy-start(f32[512]{0:T(512)S(1)} %broadcast_divide_fusion.1) | copy-start | bytes 6148
  156.3 7.8 %copy-start.6 = (s32[1,128]{1,0:T(1,128)S(1)}, s32[1,128]{1,0:T(1,128)}, u32[]{:S(2)}) copy-start(s32[1,128]{1,0:T(1,128)} %param.9) | copy-start | bytes 1540
  156.3 214.0 %all-to-all-start = ((f32[1,1024,3136]{2,0,1:T(1,128)}), f32[1,1024,3136]{2,0,1:T(1,128)}, u32[]{:S(2)}, u32[]{:S(2)}) async-start(f32[1,1024,3136]{2,0,1:T(1,128)} %copy.17), calls=%async_computation | async-start | bytes 26214400 | tf_op jit(solution)/shard_map/all_to_all | solution.py:57
  414.1 29.5 %copy-start.3 = (f32[32]{0:T(128)}, f32[32]{0:T(128)S(1)}, u32[]{:S(2)}) copy-start(f32[32]{0:T(128)S(1)} %broadcast_divide_fusion.3) | copy-start | bytes 388
  443.6 10.0 %copy-start.1 = (bf16[1,4,784,256]{3,2,1,0:T(8,128)(2,1)S(1)}, bf16[1,4,784,256]{3,2,1,0:T(8,128)(2,1)}, u32[]{:S(2)}) copy-start(bf16[1,4,784,256]{3,2,1,0:T(8,128)(2,1)} %param.8) | copy-start | bytes 4816900
Sparse Core Ops, SparseCore 0:
  10.3 42.4 all-gather.3
